TPU v7x, 32 devices: a whole 2x2x4 slice. The times are simulated.
32 devices in a mesh: groups: 2 (over y), ctx: 4 (over z), fsdp: 2 (over x), dp: 2 (over core).
Axes of the slice: x: 2, y: 2, z: 4, core: 2. Of those that a mesh axis runs over, the one named last changes fastest.
Arguments:
- query_in: bfloat16 [8, 512, 1024], P(('groups', 'fsdp', 'dp'), 'ctx'), parts along dimension 0, may hold values from -11 to 11
- key_in: bfloat16 [8, 512, 1024], P(('groups', 'fsdp', 'dp'), 'ctx'), parts along dimension 0, may hold values from -11 to 11
- value_in: bfloat16 [8, 512, 1024], P(('groups', 'fsdp', 'dp'), 'ctx'), parts along dimension 0, may hold values from -6 to 6
- utt_lengths: int32 [8], P(('groups', 'fsdp', 'dp')), parts along dimension 0, may hold values from 128 to 512, as said below
- frames_in: bfloat16 [8, 512, 1536], P(('groups', 'fsdp', 'dp'), 'ctx'), parts along dimension 0, may hold values from -6 to 6
- out_weight: bfloat16 [1024, 1536], P(None, 'fsdp'), may hold values from -1.5 to 1.5
- conv_kernel: float32 [31, 1536], P(None, 'fsdp'), may hold values from -1 to 1
- conv_bias: float32 [1536], P('fsdp'), may hold values from -3 to 3
- ln_gain: float32 [1536], P('fsdp'), may hold values from 0.1 to 1.9
- cotangent: bfloat16 [8, 512, 1536], P(('groups', 'fsdp', 'dp'), 'ctx'), parts along dimension 0, may hold values from -6 to 6
Outputs:
- block_out: bfloat16 [8, 512, 1536], P(('groups', 'fsdp', 'dp'), 'ctx'), parts along dimension 0
- hidden_grad: bfloat16 [8, 512, 1536], P(('groups', 'fsdp', 'dp'), 'ctx'), parts along dimension 0
- grad_kernel: float32 [62, 1536], P('groups', 'fsdp'), parts along dimension 0
- grad_bias: float32 [3072], P(('groups', 'fsdp')), parts along dimension 0
- grad_gain: float32 [3072], P(('groups', 'fsdp')), parts along dimension 0
There are 2 independent parts, one for each index of `groups`. A program takes and returns all parts, laid end to end along the dimension named above; an argument that names none is the same for every part. Nothing has to cross between parts.
Inputs may be any that keep to these rules, and one draw needn't show every extreme that they name: `utt_lengths`: in every group one utterance is full, of 512 valid frames.
All inputs are finite; a program needn't handle non-finite values.
Results may differ from a plain program's by a relative error of at most 0.019.
Values may be sent and summed in bfloat16 or wider, within the bound.
No kernel may reach another device: no remote copies, remote signals or barrier semaphores. Data moves between devices by JAX's collectives and lax.ppermute only.
A program may use at most 64 MiB of HBM per device.

v0:
```python
import math
import jax
import jax.numpy as jnp
from jax import lax
from jax.sharding import PartitionSpec as P

HD = 64
TAPS = 31
NEG_FILL = -1e30


def extended(block, sides, width):
    for axis, dim in sides:
        count = lax.axis_size(axis)
        forward = [(i, i + 1) for i in range(count - 1)]
        backward = [(target, source) for source, target in forward]
        low = lax.ppermute(
            lax.slice_in_dim(block, block.shape[dim] - width, None, axis=dim), axis, forward
        )
        high = lax.ppermute(lax.slice_in_dim(block, 0, width, axis=dim), axis, backward)
        block = jnp.concatenate([low, block, high], axis=dim)
    return block


def absorb_block(state, query_heads, key_heads, value_heads, key_start, valid_len):
    run_max, run_sum, summed = state
    scores = jnp.einsum(
        "qhd,khd->qhk", query_heads, key_heads, preferred_element_type=jnp.float32
    ) * (1.0 / math.sqrt(HD))
    usable = key_start + jnp.arange(key_heads.shape[0]) < valid_len
    scores = jnp.where(usable, scores, NEG_FILL)
    new_max = jnp.maximum(run_max, jnp.max(scores, axis=-1))
    rescale = jnp.exp(run_max - new_max)
    weights = jnp.where(usable, jnp.exp(scores - new_max[..., None]), 0.0)
    run_sum = run_sum * rescale + jnp.sum(weights, axis=-1)
    summed = summed * rescale[..., None] + jnp.einsum(
        "qhk,khd->qhd",
        weights.astype(jnp.bfloat16),
        value_heads,
        preferred_element_type=jnp.float32,
    )
    return (new_max, run_sum, summed)


def normalize(block):
    as_float = block.astype(jnp.float32)
    average = jnp.mean(as_float, axis=-1, keepdims=True)
    centered = as_float - average
    variance = jnp.mean(centered * centered, axis=-1, keepdims=True)
    inv_scale = lax.rsqrt(variance + 1e-05)
    return (centered * inv_scale, inv_scale)


def convolve(conv_in, kernel_all, bias_all, out_rows):
    pre_act = bias_all + jnp.zeros((out_rows, conv_in.shape[1]), jnp.float32)
    for tap_index in range(TAPS):
        pre_act = pre_act + kernel_all[tap_index] * conv_in[tap_index : tap_index + out_rows]
    return pre_act


def live_of(positions, valid_len):
    return ((positions >= 0) & (positions < valid_len)).astype(jnp.float32)[:, None]


def shards(
    query_in,
    key_in,
    value_in,
    utt_lengths,
    frames_in,
    out_weight,
    conv_kernel,
    conv_bias,
    ln_gain,
    cotangent,
):
    row_count = query_in.shape[1]
    feat_width = query_in.shape[2]
    head_count = feat_width // HD
    valid_len = utt_lengths[0]
    ctx_count = lax.axis_size("ctx")
    row_offset = lax.axis_index("ctx") * row_count
    half_taps = TAPS // 2
    query_heads = query_in[0].reshape(row_count, head_count, HD)
    start_state = (
        jnp.full((row_count, head_count), NEG_FILL, jnp.float32),
        jnp.zeros((row_count, head_count), jnp.float32),
        jnp.zeros((row_count, head_count, HD), jnp.float32),
    )
    state = start_state
    first_row = jnp.int32(0)
    key_part = lax.all_gather(key_in, "ctx", axis=1, tiled=True)
    value_part = lax.all_gather(value_in, "ctx", axis=1, tiled=True)
    piece_rows = key_part.shape[1]
    block_len = math.gcd(piece_rows, 512)
    for block_start in range(0, piece_rows, block_len):
        key_heads = key_part[0, block_start : block_start + block_len].reshape(
            block_len, head_count, HD
        )
        value_heads = value_part[0, block_start : block_start + block_len].reshape(
            block_len, head_count, HD
        )
        state = absorb_block(
            state, query_heads, key_heads, value_heads, first_row + block_start, valid_len
        )
    run_max, run_sum, summed = state
    attended = (summed / run_sum[..., None]).reshape(row_count, feat_width).astype(jnp.bfloat16)
    projected = jnp.dot(
        attended,
        lax.all_gather(out_weight, "fsdp", axis=1, tiled=True),
        preferred_element_type=jnp.float32,
    )
    hidden = (frames_in[0].astype(jnp.float32) + projected).astype(jnp.bfloat16)
    kernel_all, bias_all, gain_all = (
        lax.all_gather(conv_kernel, "fsdp", axis=1, tiled=True),
        lax.all_gather(conv_bias, "fsdp", axis=0, tiled=True),
        lax.all_gather(ln_gain, "fsdp", axis=0, tiled=True),
    )
    grad_in = cotangent[0].astype(jnp.float32)
    live_mask = live_of(row_offset + jnp.arange(row_count), valid_len)
    widened = extended(hidden, (("ctx", 0),), half_taps)
    normed_ext, inv_ext = normalize(widened)
    conv_in = (
        live_of(row_offset - half_taps + jnp.arange(row_count + 2 * half_taps), valid_len)
        * normed_ext
        * gain_all
    )
    pre_act = convolve(conv_in, kernel_all, bias_all, row_count)
    gate_val = jax.nn.sigmoid(pre_act)
    grad_pre = grad_in * live_mask * gate_val * (1.0 + pre_act * (1.0 - gate_val))
    grad_wide = extended(grad_pre.astype(jnp.bfloat16), (("ctx", 0),), half_taps).astype(
        grad_pre.dtype
    )
    normed = normed_ext[half_taps : half_taps + row_count]
    inv_scale = inv_ext[half_taps : half_taps + row_count]
    block_out = (hidden.astype(jnp.float32) + live_mask * pre_act * gate_val).astype(jnp.bfloat16)
    grad_conv = jnp.zeros((row_count, grad_pre.shape[1]), jnp.float32)
    kernel_rows = []
    for tap_index in range(TAPS):
        back = 2 * half_taps - tap_index
        grad_conv = grad_conv + kernel_all[tap_index] * grad_wide[back : back + row_count]
        kernel_rows.append(jnp.sum(grad_pre * conv_in[tap_index : tap_index + row_count], axis=0))
    grad_conv = live_mask * grad_conv
    grad_hat = grad_conv * gain_all
    first_mean = jnp.mean(grad_hat, axis=-1, keepdims=True)
    second_mean = jnp.mean(grad_hat * normed, axis=-1, keepdims=True)
    hidden_grad = (grad_in + (grad_hat - first_mean - normed * second_mean) * inv_scale).astype(
        jnp.bfloat16
    )
    factor = 1.0 / math.sqrt(lax.axis_size("fsdp") * lax.axis_size("dp") * row_count * ctx_count)
    kernel_term = jnp.stack(kernel_rows) * factor
    bias_term = (jnp.sum(grad_pre, axis=0) * factor)[None]
    gain_term = (jnp.sum(grad_conv * normed, axis=0) * factor)[None]
    shares = (
        lax.psum_scatter(
            kernel_term.astype(jnp.bfloat16), "fsdp", scatter_dimension=1, tiled=True
        ).astype(jnp.float32),
        lax.psum_scatter(
            bias_term.astype(jnp.bfloat16), "fsdp", scatter_dimension=1, tiled=True
        ).astype(jnp.float32),
        lax.psum_scatter(
            gain_term.astype(jnp.bfloat16), "fsdp", scatter_dimension=1, tiled=True
        ).astype(jnp.float32),
    )
    totals = lax.psum((shares[0], shares[1], shares[2]), ("ctx", "dp"))
    return (block_out[None], hidden_grad[None], totals[0], totals[1][0], totals[2][0])


def solution(mesh):
    in_specs = (
        P(("groups", "fsdp", "dp"), "ctx", None),
        P(("groups", "fsdp", "dp"), "ctx", None),
        P(("groups", "fsdp", "dp"), "ctx", None),
        P(("groups", "fsdp", "dp")),
        P(("groups", "fsdp", "dp"), "ctx", None),
        P(None, "fsdp"),
        P(None, "fsdp"),
        P("fsdp"),
        P("fsdp"),
        P(("groups", "fsdp", "dp"), "ctx", None),
    )
    out_specs = (
        P(("groups", "fsdp", "dp"), "ctx", None),
        P(("groups", "fsdp", "dp"), "ctx", None),
        P("groups", "fsdp"),
        P(("groups", "fsdp")),
        P(("groups", "fsdp")),
    )
    return jax.shard_map(shards, mesh=mesh, in_specs=in_specs, out_specs=out_specs, check_vma=False)
```

profile of v0, /device:TPU:0, one launch (start us, length us, event | category | flops | bytes accessed | tf_op | source)
XLA Modules:
  0.0 231.5 jit_solution(14485959095688557060)
XLA Ops:
  7.2 0.7 all-gather.6.cloned.1.call-update
  7.9 0.7 all-gather.8.cloned.1.call-update
  8.7 0.7 all-gather.10.cloned.1.call-update
  10.1 1.1 copy.24
  11.2 6.7 %all_gather.22 = f32[31,1536]{1,0:T(8,128)S(1)} all-gather(f32[31,768]{1,0:T(8,128)} %param.16), channel_id=1, replica_groups=mesh['groups'=2,'ctx'=4,'fsdp'=2,'dp'=2] {'fsdp'}, dimensions={1}, use_global_device_ids=true | all-gather | bytes 285696 | tf_op jit(solution)/shard_map/all_gather | solution.py:115
  18.4 21.8 %all-gather.6.cloned.1.call-done = bf16[1,512,1024]{2,1,0:T(8,128)(2,1)} async-done(((bf16[1,128,1024]{2,1,0:T(8,128)(2,1)}), bf16[1,512,1024]{2,1,0:T(8,128)(2,1)}) %all-gather.6.cloned.1.call-update) | async-done | bytes 1048592 | tf_op jit(solution)/shard_map/all_gather | solution.py:92
  40.2 1.5 copy.23
  41.7 27.5 %all-gather.8.cloned.1.call-done = bf16[1,512,1024]{2,1,0:T(8,128)(2,1)} async-done(((bf16[1,128,1024]{2,1,0:T(8,128)(2,1)}), bf16[1,512,1024]{2,1,0:T(8,128)(2,1)}) %all-gather.8.cloned.1.call-update) | async-done | bytes 1048592 | tf_op jit(solution)/shard_map/all_gather | solution.py:93
  69.3 1.5 copy.25
  70.8 1.1 bitcast_reduce_fusion
  71.9 1.2 fusion.2
  73.1 1.5 fusion.20
  74.6 40.7 %all-gather.10.cloned.1.call-done = bf16[1024,1536]{1,0:T(8,128)(2,1)} async-done(((bf16[1024,768]{1,0:T(8,128)(2,1)}), bf16[1024,1536]{1,0:T(8,128)(2,1)}) %all-gather.10.cloned.1.call-update) | async-done | bytes 3145744 | tf_op jit(solution)/shard_map/all_gather | solution.py:110
  115.3 2.5 %fusion.4 = bf16[128,1536]{1,0:T(8,128)(2,1)S(1)} fusion(bf16[128,1024]{0,1:T(8,128)(2,1)S(1)} %bitcast.62, bf16[1024,1536]{1,0:T(8,128)(2,1)} %all-gather.10.cloned.1.call-done, bf16[1,128,1536]{2,1,0:T(8,128)(2,1)S(1)} %copy-done.1), kind=kOutput, calls=%fused_computation.8 | convolution fusion | flops 403243008 | bytes 4194304 | tf_op jit(solution)/shard_map/dot_general | solution.py:108
  117.8 3.4 %collective-permute-start = (bf16[15,1536]{1,0:T(8,128)(2,1)S(1)}, bf16[15,1536]{1,0:T(8,128)(2,1)S(1)}, u32[]{:S(2)}, u32[]{:S(2)}) collective-permute-start(bf16[15,1536]{1,0:T(8,128)(2,1)S(1)} %get-tuple-element.82), channel_id=1, source_target_pairs={{0,4},{4,8},{8,12},{1,5},{5,9},{9,13},{2,6},{6,10},{10,14},{3,7},{... | collective-permute-start | bytes 138248 | tf_op jit(solution)/shard_map/ppermute | solution.py:17
  121.2 1.3 collective-permute-start.1
  122.5 4.3 %all-gather.1 = f32[2,1,768]{2,1,0:T(1,128)S(1)} all-gather(f32[1,1,768]{2,1,0:T(1,128)S(1)} %reshape.114), channel_id=1, replica_groups=mesh['groups'=2,'ctx'=4,'fsdp'=2,'dp'=2] {'fsdp'}, dimensions={0}, use_global_device_ids=true | all-gather | bytes 9216 | tf_op jit(solution)/shard_map/all_gather | solution.py:117
  126.9 4.3 %all-gather = f32[2,1,768]{2,1,0:T(1,128)S(1)} all-gather(f32[1,1,768]{2,1,0:T(1,128)S(1)} %reshape.112), channel_id=1, replica_groups=mesh['groups'=2,'ctx'=4,'fsdp'=2,'dp'=2] {'fsdp'}, dimensions={0}, use_global_device_ids=true | all-gather | bytes 9216 | tf_op jit(solution)/shard_map/all_gather | solution.py:116
  131.6 0.3 fusion.23
  131.9 0.3 fusion.15
  132.3 6.3 %multiply_reduce_fusion.1 = (f32[1536]{0:T(1024)S(1)}, f32[1536]{0:T(1024)S(1)}, f32[1536]{0:T(1024)S(1)}, f32[1536]{0:T(1024)S(1)}, f32[1536]{0:T(1024)S(1)}, /...) fusion(f32[158,1536]{1,0:T(8,128)S(1)} %get-tuple-element.79, ...), kind=kLoop, calls=%fused_computation.90 | loop fusion | flops 21206016 | bytes 26653184 | tf_op jit(solution)/shard_map/reduce_sum | solution.py:142
  138.6 2.1 multiply_reduce_fusion.19
  140.8 4.5 %collective-permute-start.2 = (bf16[15,1536]{1,0:T(8,128)(2,1)S(1)}, bf16[15,1536]{1,0:T(8,128)(2,1)S(1)}, u32[]{:S(2)}, u32[]{:S(2)}) collective-permute-start(bf16[15,1536]{1,0:T(8,128)(2,1)S(1)} %get-tuple-element.80), channel_id=1, source_target_pairs={{0,4},{4,8},{8,12},{1,5},{5,9},{9,13},{2,6},{6,10},{10,14},{3,7},{... | collective-permute-start | bytes 138248 | tf_op jit(solution)/shard_map/ppermute | solution.py:17
  145.3 1.3 collective-permute-start.3
  146.6 1.0 reshape_bitcast_fusion.1
  147.9 1.7 fusion.59
  149.6 0.7 stack.100
  150.3 0.7 stack.101
  151.0 0.7 stack.102
  151.7 0.7 stack.103
  152.4 0.7 stack.104
  153.1 0.7 stack.105
  153.8 0.7 stack.106
  154.5 0.7 stack.107
  155.2 0.7 stack.108
  155.9 0.7 stack.96
  156.6 0.7 stack.97
  157.3 0.7 stack.98
  158.0 0.7 stack.99
  159.4 6.1 %multiply_reduce_fusion = (f32[1536]{0:T(1024)S(1)}, f32[128]{0:T(128)S(1)}, f32[128]{0:T(128)S(1)}, f32[128,1536]{1,0:T(8,128)S(1)}) fusion(f32[158,1536]{1,0:T(8,128)S(1)} %get-tuple-element.78, f32[1536]{0:T(1024)S(1)} %reshape.115, f32[158,1536]{1,0:T(8,128)S(1)} %maximum_convert_fusion, f32[1536]{0:T(1024)S(1)} %get-tuple-element.41, ...), kind=kLoop, calls=%fused_computation.89 | loop fusion | flops 13367552 | bytes 26156544 | tf_op jit(solution)/shard_map/reduce_sum | solution.py:153
  165.6 1.0 reshape_bitcast_fusion
  166.6 0.7 multiply_convert_fusion
  167.4 1.0 copy.29
  168.5 1.1 fusion.58
  169.5 11.5 %reduce-scatter.12.cloned.1.call-done = bf16[768,1]{1,0:T(8,128)(2,1)} async-done(((bf16[1536,1]{1,0:T(8,128)(2,1)}), bf16[768,1]{1,0:T(8,128)(2,1)}) %reduce-scatter.12.cloned.1.call-update) | async-done | bytes 1552
  181.0 1.0 copy.31
  182.1 11.6 %reduce-scatter.8.cloned.1.call-done = bf16[31,768]{1,0:T(8,128)(2,1)} async-done(((bf16[31,1536]{1,0:T(8,128)(2,1)}), bf16[31,768]{1,0:T(8,128)(2,1)}) %reduce-scatter.8.cloned.1.call-update) | async-done | bytes 47632 | tf_op jit(solution)/shard_map/reduce_scatter | solution.py:155
  193.7 31.0 %all-reduce.2 = (f32[31,768]{1,0:T(8,128)}, f32[768]{0:T(1024)}, f32[768]{0:T(1024)}) all-reduce(bf16[31,768]{1,0:T(8,128)(2,1)} %reduce-scatter.8.cloned.1.call-done, f32[768]{0:T(1024)S(1)} %get-tuple-element.91, f32[768]{0:T(1024)S(1)} %get-tuple-element.90), channel_id=1, replica_groups=mesh['groups'=2,'ctx'=4,'fsdp'=2,'dp'=2] {'ctx','dp'}, use_global_device_ids=true, to_apply=%region_38.39 | all-reduce | flops 25344 | bytes 155136 | tf_op jit(solution)/shard_map/psum | solution.py:165
  (71 shorter events, 2.1 us)
Async XLA Ops:
  7.2 33.1 %all-gather.6.cloned.1.call-start = ((), (), s32[]{:S(2)}) async-start(), calls=%async_computation.3 | async-start | bytes 1310720 | tf_op jit(solution)/shard_map/all_gather | solution.py:92
  7.9 61.4 %all-gather.8.cloned.1.call-start = ((), (), s32[]{:S(2)}) async-start(), calls=%async_computation.4 | async-start | bytes 1310720 | tf_op jit(solution)/shard_map/all_gather | solution.py:93
  8.6 106.6 %all-gather.10.cloned.1.call-start = ((), (), s32[]{:S(2)}) async-start(), calls=%async_computation.5 | async-start | bytes 4718592 | tf_op jit(solution)/shard_map/all_gather | solution.py:110
  9.4 158.0 %reduce-scatter.10.cloned.1.call-start = ((), (), s32[]{:S(2)}) async-start(), calls=%async_computation.7 | async-start | bytes 589824
  73.1 42.2 %copy-start.1 = (bf16[1,128,1536]{2,1,0:T(8,128)(2,1)S(1)}, bf16[1,128,1536]{2,1,0:T(8,128)(2,1)}, u32[]{:S(2)}) copy-start(bf16[1,128,1536]{2,1,0:T(8,128)(2,1)} %param.14) | copy-start | bytes 1179652
  74.5 48.0 %copy-start.5 = (f32[768]{0:T(1024)S(1)}, f32[768]{0:T(1024)}, u32[]{:S(2)}) copy-start(f32[768]{0:T(1024)} %param.18) | copy-start | bytes 9220
  74.5 52.4 %copy-start.6 = (f32[768]{0:T(1024)S(1)}, f32[768]{0:T(1024)}, u32[]{:S(2)}) copy-start(f32[768]{0:T(1024)} %param.17) | copy-start | bytes 9220
  74.6 57.7 %copy-start = (bf16[1,128,1536]{2,1,0:T(8,128)(2,1)S(1)}, bf16[1,128,1536]{2,1,0:T(8,128)(2,1)}, u32[]{:S(2)}) copy-start(bf16[1,128,1536]{2,1,0:T(8,128)(2,1)} %param.19) | copy-start | bytes 1179652
  117.8 13.5 %collective-permute-start = (bf16[15,1536]{1,0:T(8,128)(2,1)S(1)}, bf16[15,1536]{1,0:T(8,128)(2,1)S(1)}, u32[]{:S(2)}, u32[]{:S(2)}) collective-permute-start(bf16[15,1536]{1,0:T(8,128)(2,1)S(1)} %get-tuple-element.82), channel_id=1, source_target_pairs={{0,4},{4,8},{8,12},{1,5},{5,9},{9,13},{2,6},{6,10},{10,14},{3,7},{... | collective-permute-start | bytes 138248 | tf_op jit(solution)/shard_map/ppermute | solution.py:17
  121.2 10.1 %collective-permute-start.1 = (bf16[15,1536]{1,0:T(8,128)(2,1)S(1)}, bf16[15,1536]{1,0:T(8,128)(2,1)S(1)}, u32[]{:S(2)}, u32[]{:S(2)}) collective-permute-start(bf16[15,1536]{1,0:T(8,128)(2,1)S(1)} %get-tuple-element.83), channel_id=1, source_target_pairs={{4,0},{8,4},{12,8},{5,1},{9,5},{13,9},{6,2},{10,6},{14,10},{7,3},{... | collective-permute-start | bytes 138248 | tf_op jit(solution)/shard_map/ppermute | solution.py:20
  122.5 16.1 %copy-start.2 = (f32[128]{0:T(128)}, f32[128]{0:T(128)S(1)}, u32[]{:S(2)}) copy-start(f32[128]{0:T(128)S(1)} %and_convert_fusion.1) | copy-start | bytes 1540
  131.9 6.7 %copy-start.3 = (f32[158]{0:T(256)}, f32[158]{0:T(256)S(1)}, u32[]{:S(2)}) copy-start(f32[158]{0:T(256)S(1)} %add_rsqrt_fusion) | copy-start | bytes 1900
  140.8 18.5 %collective-permute-start.2 = (bf16[15,1536]{1,0:T(8,128)(2,1)S(1)}, bf16[15,1536]{1,0:T(8,128)(2,1)S(1)}, u32[]{:S(2)}, u32[]{:S(2)}) collective-permute-start(bf16[15,1536]{1,0:T(8,128)(2,1)S(1)} %get-tuple-element.80), channel_id=1, source_target_pairs={{0,4},{4,8},{8,12},{1,5},{5,9},{9,13},{2,6},{6,10},{10,14},{3,7},{... | collective-permute-start | bytes 138248 | tf_op jit(solution)/shard_map/ppermute | solution.py:17
  145.3 14.0 %collective-permute-start.3 = (bf16[15,1536]{1,0:T(8,128)(2,1)S(1)}, bf16[15,1536]{1,0:T(8,128)(2,1)S(1)}, u32[]{:S(2)}, u32[]{:S(2)}) collective-permute-start(bf16[15,1536]{1,0:T(8,128)(2,1)S(1)} %get-tuple-element.81), channel_id=1, source_target_pairs={{4,0},{8,4},{12,8},{5,1},{9,5},{13,9},{6,2},{10,6},{14,10},{7,3},{... | collective-permute-start | bytes 138248 | tf_op jit(solution)/shard_map/ppermute | solution.py:20
  147.7 33.4 %reduce-scatter.12.cloned.1.call-start = ((), (), s32[]{:S(2)}) async-start(), calls=%async_computation.8 | async-start | bytes 589824
  159.4 7.9 %copy-start.4 = (f32[158]{0:T(256)S(1)}, f32[158]{0:T(256)}, u32[]{:S(2)}) copy-start(f32[158]{0:T(256)} %copy-done.3) | copy-start | bytes 1900
  166.6 27.1 %reduce-scatter.8.cloned.1.call-start = ((), (), s32[]{:S(2)}) async-start(), calls=%async_computation.6 | async-start | bytes 147456 | tf_op jit(solution)/shard_map/reduce_scatter | solution.py:155
Sparse Core Ops, SparseCore 0:
  9.6 30.6 all-gather.5
  41.8 27.4 all-gather.7
  70.8 44.4 all-gather.9
  147.8 14.2 reduce-scatter.9
  166.7 14.2 reduce-scatter.11
  183.6 9.9 reduce-scatter.7
where the time goes:
time: 233 us; the launch traced here: 232 us
  waiting for transfers between devices  115 us (49%)
  blocking collectives  46.4 us (20%)
  other arithmetic  20.3 us (9%)
  local copies, waits for them, and re-layouts  18.4 us (8%)
  between operations  15.2 us (7%)
  starting transfers between devices  10.9 us (5%)
  matrix products  5.07 us (2%)
    all_gather x1, waiting for transfers between devices, shards(): lax.all_gather(out_weight, 'fsdp', axis=1, tiled=True)  40.7 us
    psum x1, blocking collectives, shards(): totals = lax.psum((shares[0], shares[1], shares[2]), ('ctx', 'dp'))  31 us
    all_gather x1, waiting for transfers between devices, shards(): value_part = lax.all_gather(value_in, 'ctx', axis=1, tiled=True)  27.5 us
    all_gather x1, waiting for transfers between devices, shards(): key_part = lax.all_gather(key_in, 'ctx', axis=1, tiled=True)  21.8 us
    unnamed x8, waiting for transfers between devices  13.6 us
    reduce_scatter x1, waiting for transfers between devices, shards(): lax.psum_scatter(kernel_term.astype(jnp.bfloat16), 'fsdp', scatter_dimens...  11.6 us
    another operation x32, local copies, waits for them, and re-layouts, shards(): kernel_term = jnp.stack(kernel_rows) * factor  9.55 us
    reduce_sum x2, other arithmetic, shards(): jnp.sum(grad_pre * conv_in[tap_index:tap_index + row_count], axis=0)  8.42 us
  transfers between devices with their start and end apart: 10, of which 5 were waited for; matrix products, arithmetic and copies ran while one was open for 14% of the time, Pallas kernels for 0%

commit v1 on v0

--- a/solution.py
+++ b/solution.py
@@ -162,7 +162,7 @@
             gain_term.astype(jnp.bfloat16), "fsdp", scatter_dimension=1, tiled=True
         ).astype(jnp.float32),
     )
-    totals = lax.psum((shares[0], shares[1], shares[2]), ("ctx", "dp"))
+    totals = lax.psum(lax.psum((shares[0], shares[1], shares[2]), "dp"), "ctx")
     return (block_out[None], hidden_grad[None], totals[0], totals[1][0], totals[2][0])
 
 

time: 233 us -> 243 us (1.043)
  waiting for transfers between devices: 115 us -> 137 us
  blocking collectives: 46.4 us -> 32.8 us
    psum x0 -> x1, waiting for transfers between devices: none -> 21 us  [shards(): totals = lax.psum(lax.psum((shares[0], shares[1], shares[2]), 'dp'), 'ctx')]
    psum x1 -> x2, blocking collectives: 31 us -> 17.4 us  [shards(): totals = lax.psum(lax.psum((shares[0], shares[1], shares[2]), 'dp'), 'ctx')]
    unnamed x23 -> x24, local copies, waits for them, and re-layouts: 5.28 us -> 7.03 us
    unnamed x8 -> x9, waiting for transfers between devices: 13.6 us -> 14.6 us
  transfers between devices with their start and end apart: 10 -> 11, of which waited for: 5 -> 6; matrix products, arithmetic and copies ran while one was open for 14% -> 13% of each run, Pallas kernels for 0% -> 0%
where the time goes in v1:
time: 243 us; the launch traced here: 242 us
  waiting for transfers between devices  137 us (56%)
  blocking collectives  32.8 us (13%)
  local copies, waits for them, and re-layouts  20.2 us (8%)
  other arithmetic  20.2 us (8%)
  between operations  15.2 us (6%)
  starting transfers between devices  11 us (5%)
  matrix products  5.07 us (2%)
    all_gather x1, waiting for transfers between devices, shards(): lax.all_gather(out_weight, 'fsdp', axis=1, tiled=True)  40.7 us
    all_gather x1, waiting for transfers between devices, shards(): value_part = lax.all_gather(value_in, 'ctx', axis=1, tiled=True)  27.5 us
    all_gather x1, waiting for transfers between devices, shards(): key_part = lax.all_gather(key_in, 'ctx', axis=1, tiled=True)  21.8 us
    psum x1, waiting for transfers between devices, shards(): totals = lax.psum(lax.psum((shares[0], shares[1], shares[2]), 'dp'), 'ctx')  21 us
    psum x2, blocking collectives, shards(): totals = lax.psum(lax.psum((shares[0], shares[1], shares[2]), 'dp'), 'ctx')  17.4 us
    unnamed x9, waiting for transfers between devices  14.6 us
    reduce_scatter x1, waiting for transfers between devices, shards(): lax.psum_scatter(kernel_term.astype(jnp.bfloat16), 'fsdp', scatter_dimens...  11.6 us
    another operation x32, local copies, waits for them, and re-layouts, shards(): kernel_term = jnp.stack(kernel_rows) * factor  9.55 us
  transfers between devices with their start and end apart: 11, of which 6 were waited for; matrix products, arithmetic and copies ran while one was open for 13% of the time, Pallas kernels for 0%

profile of v1, /device:TPU:0, one launch (start us, length us, event | category | flops | bytes accessed | tf_op | source)
XLA Modules:
  0.0 241.7 jit_solution(15445005633551037964)
XLA Ops:
  7.2 0.7 all-gather.6.cloned.1.call-update
  7.9 0.7 all-gather.8.cloned.1.call-update
  8.7 0.7 all-gather.10.cloned.1.call-update
  10.1 1.1 copy.24
  11.2 6.7 %all_gather.22 = f32[31,1536]{1,0:T(8,128)S(1)} all-gather(f32[31,768]{1,0:T(8,128)} %param.16), channel_id=1, replica_groups=mesh['groups'=2,'ctx'=4,'fsdp'=2,'dp'=2] {'fsdp'}, dimensions={1}, use_global_device_ids=true | all-gather | bytes 285696 | tf_op jit(solution)/shard_map/all_gather | solution.py:115
  18.4 21.8 %all-gather.6.cloned.1.call-done = bf16[1,512,1024]{2,1,0:T(8,128)(2,1)} async-done(((bf16[1,128,1024]{2,1,0:T(8,128)(2,1)}), bf16[1,512,1024]{2,1,0:T(8,128)(2,1)}) %all-gather.6.cloned.1.call-update) | async-done | bytes 1048592 | tf_op jit(solution)/shard_map/all_gather | solution.py:92
  40.2 1.5 copy.23
  41.7 27.5 %all-gather.8.cloned.1.call-done = bf16[1,512,1024]{2,1,0:T(8,128)(2,1)} async-done(((bf16[1,128,1024]{2,1,0:T(8,128)(2,1)}), bf16[1,512,1024]{2,1,0:T(8,128)(2,1)}) %all-gather.8.cloned.1.call-update) | async-done | bytes 1048592 | tf_op jit(solution)/shard_map/all_gather | solution.py:93
  69.3 1.5 copy.25
  70.8 1.1 bitcast_reduce_fusion
  71.9 1.1 fusion.2
  73.1 1.5 fusion.20
  74.5 40.7 %all-gather.10.cloned.1.call-done = bf16[1024,1536]{1,0:T(8,128)(2,1)} async-done(((bf16[1024,768]{1,0:T(8,128)(2,1)}), bf16[1024,1536]{1,0:T(8,128)(2,1)}) %all-gather.10.cloned.1.call-update) | async-done | bytes 3145744 | tf_op jit(solution)/shard_map/all_gather | solution.py:110
  115.3 2.5 %fusion.4 = bf16[128,1536]{1,0:T(8,128)(2,1)S(1)} fusion(bf16[128,1024]{0,1:T(8,128)(2,1)S(1)} %bitcast.62, bf16[1024,1536]{1,0:T(8,128)(2,1)} %all-gather.10.cloned.1.call-done, bf16[1,128,1536]{2,1,0:T(8,128)(2,1)S(1)} %copy-done.1), kind=kOutput, calls=%fused_computation.8 | convolution fusion | flops 403243008 | bytes 4194304 | tf_op jit(solution)/shard_map/dot_general | solution.py:108
  117.8 3.4 %collective-permute-start = (bf16[15,1536]{1,0:T(8,128)(2,1)S(1)}, bf16[15,1536]{1,0:T(8,128)(2,1)S(1)}, u32[]{:S(2)}, u32[]{:S(2)}) collective-permute-start(bf16[15,1536]{1,0:T(8,128)(2,1)S(1)} %get-tuple-element.84), channel_id=1, source_target_pairs={{0,4},{4,8},{8,12},{1,5},{5,9},{9,13},{2,6},{6,10},{10,14},{3,7},{... | collective-permute-start | bytes 138248 | tf_op jit(solution)/shard_map/ppermute | solution.py:17
  121.2 1.3 collective-permute-start.1
  122.5 4.3 %all-gather.1 = f32[2,1,768]{2,1,0:T(1,128)S(1)} all-gather(f32[1,1,768]{2,1,0:T(1,128)S(1)} %reshape.114), channel_id=1, replica_groups=mesh['groups'=2,'ctx'=4,'fsdp'=2,'dp'=2] {'fsdp'}, dimensions={0}, use_global_device_ids=true | all-gather | bytes 9216 | tf_op jit(solution)/shard_map/all_gather | solution.py:117
  126.9 4.3 %all-gather = f32[2,1,768]{2,1,0:T(1,128)S(1)} all-gather(f32[1,1,768]{2,1,0:T(1,128)S(1)} %reshape.112), channel_id=1, replica_groups=mesh['groups'=2,'ctx'=4,'fsdp'=2,'dp'=2] {'fsdp'}, dimensions={0}, use_global_device_ids=true | all-gather | bytes 9216 | tf_op jit(solution)/shard_map/all_gather | solution.py:116
  132.5 6.3 %multiply_reduce_fusion.1 = (f32[1536]{0:T(1024)S(1)}, f32[1536]{0:T(1024)S(1)}, f32[1536]{0:T(1024)S(1)}, f32[1536]{0:T(1024)S(1)}, f32[1536]{0:T(1024)S(1)}, /...) fusion(f32[158,1536]{1,0:T(8,128)S(1)} %get-tuple-element.81, ...), kind=kLoop, calls=%fused_computation.90 | loop fusion | flops 21206016 | bytes 26653184 | tf_op jit(solution)/shard_map/reduce_sum | solution.py:142
  138.8 2.1 multiply_reduce_fusion.19
  140.9 4.5 %collective-permute-start.2 = (bf16[15,1536]{1,0:T(8,128)(2,1)S(1)}, bf16[15,1536]{1,0:T(8,128)(2,1)S(1)}, u32[]{:S(2)}, u32[]{:S(2)}) collective-permute-start(bf16[15,1536]{1,0:T(8,128)(2,1)S(1)} %get-tuple-element.82), channel_id=1, source_target_pairs={{0,4},{4,8},{8,12},{1,5},{5,9},{9,13},{2,6},{6,10},{10,14},{3,7},{... | collective-permute-start | bytes 138248 | tf_op jit(solution)/shard_map/ppermute | solution.py:17
  145.5 1.3 collective-permute-start.3
  146.8 1.0 reshape_bitcast_fusion.1
  148.0 1.7 fusion.59
  149.7 0.7 stack.100
  150.4 0.7 stack.101
  151.1 0.7 stack.102
  151.8 0.7 stack.103
  152.5 0.7 stack.104
  153.2 0.7 stack.105
  153.9 0.7 stack.106
  154.6 0.7 stack.107
  155.3 0.7 stack.108
  156.0 0.7 stack.96
  156.7 0.7 stack.97
  157.4 0.7 stack.98
  158.1 0.7 stack.99
  159.6 6.1 %multiply_reduce_fusion = (f32[1536]{0:T(1024)S(1)}, f32[128]{0:T(128)S(1)}, f32[128]{0:T(128)S(1)}, f32[128,1536]{1,0:T(8,128)S(1)}) fusion(f32[158,1536]{1,0:T(8,128)S(1)} %get-tuple-element.80, f32[1536]{0:T(1024)S(1)} %reshape.115, f32[158,1536]{1,0:T(8,128)S(1)} %maximum_convert_fusion, f32[1536]{0:T(1024)S(1)} %get-tuple-element.41, ...), kind=kLoop, calls=%fused_computation.89 | loop fusion | flops 13367552 | bytes 26156544 | tf_op jit(solution)/shard_map/reduce_sum | solution.py:153
  165.7 1.0 reshape_bitcast_fusion
  167.6 1.0 copy.29
  168.7 12.5 %reduce-scatter.12.cloned.1.call-done = bf16[768,1]{1,0:T(8,128)(2,1)} async-done(((bf16[1536,1]{1,0:T(8,128)(2,1)}), bf16[768,1]{1,0:T(8,128)(2,1)}) %reduce-scatter.12.cloned.1.call-update) | async-done | bytes 1552
  181.2 1.0 copy.31
  182.2 11.6 %reduce-scatter.8.cloned.1.call-done = bf16[31,768]{1,0:T(8,128)(2,1)} async-done(((bf16[31,1536]{1,0:T(8,128)(2,1)}), bf16[31,768]{1,0:T(8,128)(2,1)}) %reduce-scatter.8.cloned.1.call-update) | async-done | bytes 47632 | tf_op jit(solution)/shard_map/reduce_scatter | solution.py:155
  193.8 5.0 %all-reduce.6 = (f32[31,768]{1,0:T(8,128)}, f32[1,768]{1,0:T(1,128)S(1)}, f32[1,768]{1,0:T(1,128)S(1)}) all-reduce(bf16[31,768]{1,0:T(8,128)(2,1)} %reduce-scatter.8.cloned.1.call-done, bf16[1,768]{1,0:T(2,128)(2,1)S(1)} %copy.29, bf16[1,768]{1,0:T(2,128)(2,1)S(1)} %copy.31), channel_id=1, replica_groups=mesh['groups'=2,'ctx'=4,'fsdp'=2,'dp'=2] {'dp'}, use_global_device_ids=true, to_apply=%region_38.39 | all-reduce | flops 25344 | bytes 152064 | tf_op jit(solution)/shard_map/psum | solution.py:165
  198.8 1.1 fusion.58
  199.9 12.5 %all-reduce = (f32[768]{0:T(1024)}, f32[768]{0:T(1024)}) all-reduce(f32[768]{0:T(1024)S(1)} %reduce.33, f32[768]{0:T(1024)S(1)} %reduce.34), channel_id=1, replica_groups=mesh['groups'=2,'ctx'=4,'fsdp'=2,'dp'=2] {'ctx'}, use_global_device_ids=true, to_apply=%region_43.44 | all-reduce | flops 1536 | bytes 12288 | tf_op jit(solution)/shard_map/psum | solution.py:165
  212.4 21.0 %all-reduce.5.cloned.1.call-done = f32[31,768]{1,0:T(8,128)} async-done(((f32[31,768]{1,0:T(8,128)}), f32[31,768]{1,0:T(8,128)}) %all-reduce.5.cloned.1.call-update) | async-done | bytes 95248 | tf_op jit(solution)/shard_map/psum | solution.py:165
  233.3 1.5 copy.40
  (77 shorter events, 3.7 us)
Async XLA Ops:
  7.2 33.1 %all-gather.6.cloned.1.call-start = ((), (), s32[]{:S(2)}) async-start(), calls=%async_computation.3 | async-start | bytes 1310720 | tf_op jit(solution)/shard_map/all_gather | solution.py:92
  7.9 61.4 %all-gather.8.cloned.1.call-start = ((), (), s32[]{:S(2)}) async-start(), calls=%async_computation.4 | async-start | bytes 1310720 | tf_op jit(solution)/shard_map/all_gather | solution.py:93
  8.6 106.6 %all-gather.10.cloned.1.call-start = ((), (), s32[]{:S(2)}) async-start(), calls=%async_computation.5 | async-start | bytes 4718592 | tf_op jit(solution)/shard_map/all_gather | solution.py:110
  9.4 158.2 %reduce-scatter.10.cloned.1.call-start = ((), (), s32[]{:S(2)}) async-start(), calls=%async_computation.8 | async-start | bytes 589824
  73.0 42.2 %copy-start.1 = (bf16[1,128,1536]{2,1,0:T(8,128)(2,1)S(1)}, bf16[1,128,1536]{2,1,0:T(8,128)(2,1)}, u32[]{:S(2)}) copy-start(bf16[1,128,1536]{2,1,0:T(8,128)(2,1)} %param.14) | copy-start | bytes 1179652
  74.5 48.0 %copy-start.5 = (f32[768]{0:T(1024)S(1)}, f32[768]{0:T(1024)}, u32[]{:S(2)}) copy-start(f32[768]{0:T(1024)} %param.18) | copy-start | bytes 9220
  74.5 52.4 %copy-start.6 = (f32[768]{0:T(1024)S(1)}, f32[768]{0:T(1024)}, u32[]{:S(2)}) copy-start(f32[768]{0:T(1024)} %param.17) | copy-start | bytes 9220
  74.5 58.0 %copy-start = (bf16[1,128,1536]{2,1,0:T(8,128)(2,1)S(1)}, bf16[1,128,1536]{2,1,0:T(8,128)(2,1)}, u32[]{:S(2)}) copy-start(bf16[1,128,1536]{2,1,0:T(8,128)(2,1)} %param.19) | copy-start | bytes 1179652
  117.8 13.5 %collective-permute-start = (bf16[15,1536]{1,0:T(8,128)(2,1)S(1)}, bf16[15,1536]{1,0:T(8,128)(2,1)S(1)}, u32[]{:S(2)}, u32[]{:S(2)}) collective-permute-start(bf16[15,1536]{1,0:T(8,128)(2,1)S(1)} %get-tuple-element.84), channel_id=1, source_target_pairs={{0,4},{4,8},{8,12},{1,5},{5,9},{9,13},{2,6},{6,10},{10,14},{3,7},{... | collective-permute-start | bytes 138248 | tf_op jit(solution)/shard_map/ppermute | solution.py:17
  121.2 10.1 %collective-permute-start.1 = (bf16[15,1536]{1,0:T(8,128)(2,1)S(1)}, bf16[15,1536]{1,0:T(8,128)(2,1)S(1)}, u32[]{:S(2)}, u32[]{:S(2)}) collective-permute-start(bf16[15,1536]{1,0:T(8,128)(2,1)S(1)} %get-tuple-element.85), channel_id=1, source_target_pairs={{4,0},{8,4},{12,8},{5,1},{9,5},{13,9},{6,2},{10,6},{14,10},{7,3},{... | collective-permute-start | bytes 138248 | tf_op jit(solution)/shard_map/ppermute | solution.py:20
  122.5 16.2 %copy-start.2 = (f32[128]{0:T(128)}, f32[128]{0:T(128)S(1)}, u32[]{:S(2)}) copy-start(f32[128]{0:T(128)S(1)} %and_convert_fusion.1) | copy-start | bytes 1540
  131.9 0.6 copy-start.3
  140.9 18.5 %collective-permute-start.2 = (bf16[15,1536]{1,0:T(8,128)(2,1)S(1)}, bf16[15,1536]{1,0:T(8,128)(2,1)S(1)}, u32[]{:S(2)}, u32[]{:S(2)}) collective-permute-start(bf16[15,1536]{1,0:T(8,128)(2,1)S(1)} %get-tuple-element.82), channel_id=1, source_target_pairs={{0,4},{4,8},{8,12},{1,5},{5,9},{9,13},{2,6},{6,10},{10,14},{3,7},{... | collective-permute-start | bytes 138248 | tf_op jit(solution)/shard_map/ppermute | solution.py:17
  145.5 14.0 %collective-permute-start.3 = (bf16[15,1536]{1,0:T(8,128)(2,1)S(1)}, bf16[15,1536]{1,0:T(8,128)(2,1)S(1)}, u32[]{:S(2)}, u32[]{:S(2)}) collective-permute-start(bf16[15,1536]{1,0:T(8,128)(2,1)S(1)} %get-tuple-element.83), channel_id=1, source_target_pairs={{4,0},{8,4},{12,8},{5,1},{9,5},{13,9},{6,2},{10,6},{14,10},{7,3},{... | collective-permute-start | bytes 138248 | tf_op jit(solution)/shard_map/ppermute | solution.py:20
  147.8 33.4 %reduce-scatter.12.cloned.1.call-start = ((), (), s32[]{:S(2)}) async-start(), calls=%async_computation.9 | async-start | bytes 589824
  159.6 7.9 %copy-start.4 = (f32[158]{0:T(256)S(1)}, f32[158]{0:T(256)}, u32[]{:S(2)}) copy-start(f32[158]{0:T(256)} %copy-done.3) | copy-start | bytes 1900
  166.7 27.1 %reduce-scatter.8.cloned.1.call-start = ((), (), s32[]{:S(2)}) async-start(), calls=%async_computation.6 | async-start | bytes 147456 | tf_op jit(solution)/shard_map/reduce_scatter | solution.py:155
  167.5 65.8 %all-reduce.5.cloned.1.call-start = ((), (), s32[]{:S(2)}) async-start(), calls=%async_computation.7 | async-start | bytes 196608 | tf_op jit(solution)/shard_map/psum | solution.py:165
Sparse Core Ops, SparseCore 0:
  9.6 30.6 all-gather.5
  41.8 27.4 all-gather.7
  70.8 44.4 all-gather.9
  147.9 14.2 reduce-scatter.9
  166.9 14.2 reduce-scatter.11
  183.8 9.9 reduce-scatter.7
  198.9 34.3 all-reduce.4
